TPU v7x, 32 devices: a whole 2x2x4 slice. The times are simulated.
32 devices in a mesh: parts: 1, row: 16 (over z, y, x), chan: 1, sub: 2 (over core).
Axes of the slice: x: 2, y: 2, z: 4, core: 2. Of those that a mesh axis runs over, the one named last changes fastest.
Arguments:
- pair: bfloat16 [448, 448, 128], P(('parts', 'row', 'sub'), 'chan'), may hold values from -6 to 6
- pair_mask: int32 [448, 448], P(('parts', 'row', 'sub'), 'chan'), may hold values 0 or 1
- out_in_gain: float32 [128], replicated, may hold values from 0.5 to 1.5
- out_proj: bfloat16 [128, 640], replicated, may hold values from -0.5 to 0.5
- out_mid_gain: float32 [128], replicated, may hold values from 0.5 to 1.5
- out_final: bfloat16 [128, 128], replicated, may hold values from -0.5 to 0.5
- in_in_gain: float32 [128], replicated, may hold values from 0.5 to 1.5
- in_proj: bfloat16 [128, 640], replicated, may hold values from -0.5 to 0.5
- in_mid_gain: float32 [128], replicated, may hold values from 0.5 to 1.5
- in_final: bfloat16 [128, 128], replicated, may hold values from -0.5 to 0.5
Outputs:
- updated: bfloat16 [448, 448, 128], P(('parts', 'row', 'sub'), 'chan')
All inputs are finite; a program needn't handle non-finite values. No bound on the sum of `pair_mask` on one device may be relied on, other than what follows from the above.
Results may differ from a plain program's by a relative error of at most 0.014.
Values may be sent and summed in bfloat16 or wider, within the bound.
A program may use at most 192 MiB of HBM per device.

v0:
```python
import jax
import jax.numpy as jnp
from jax import lax
from jax.sharding import PartitionSpec as P


def norm_last(values, gain):
    mean = jnp.mean(values, axis=-1, keepdims=True)
    var = jnp.mean((values - mean) ** 2, axis=-1, keepdims=True)
    return (values - mean) / jnp.sqrt(var + 1e-05) * gain


def project(pair, pair_mask, in_gain, proj, left_form, right_form, left_across):
    hidden = (proj.shape[1] - pair.shape[2]) // 4
    normed = norm_last(pair.astype(jnp.float32), in_gain).astype(jnp.bfloat16)
    keep = pair_mask.astype(jnp.float32)
    left_raw = jnp.einsum(
        left_form, normed, proj[:, : 2 * hidden], preferred_element_type=jnp.float32
    )
    right_raw = jnp.einsum(
        right_form, normed, proj[:, 2 * hidden : 4 * hidden], preferred_element_type=jnp.float32
    )
    left_keep = keep.T[None] if left_across else keep[None]
    left = (jax.nn.sigmoid(left_raw[:hidden]) * left_raw[hidden:] * left_keep).astype(jnp.bfloat16)
    right = (jax.nn.sigmoid(right_raw[:hidden]) * right_raw[hidden:] * keep[None]).astype(
        jnp.bfloat16
    )
    gate = jax.nn.sigmoid(
        jnp.dot(normed, proj[:, 4 * hidden :], preferred_element_type=jnp.float32)
    )
    return (left, right, gate)


def finish(pair, product, gate, mid_gain, final):
    group = product.shape[0]
    total = group * lax.axis_size("chan")
    first, second = (
        lax.psum(jnp.sum(product, axis=0).astype(jnp.bfloat16), "chan").astype(jnp.float32),
        lax.psum(jnp.sum(product * product, axis=0).astype(jnp.bfloat16), "chan").astype(
            jnp.float32
        ),
    )
    mean = first / total
    var = second / total - mean * mean
    offset = lax.axis_index("chan") * group
    gain_part = lax.dynamic_slice_in_dim(mid_gain, offset, group, 0)
    final_part = lax.dynamic_slice_in_dim(final, offset, group, 0)
    normed = ((product - mean) / jnp.sqrt(var + 1e-05) * gain_part[:, None, None]).astype(
        jnp.bfloat16
    )
    summed = lax.psum_scatter(
        jnp.einsum("crj,cd->jrd", normed, final_part, preferred_element_type=jnp.float32).astype(
            jnp.bfloat16
        ),
        "chan",
        scatter_dimension=0,
        tiled=True,
    ).astype(jnp.float32)
    update = jnp.transpose(summed, (1, 0, 2))
    return (pair.astype(jnp.float32) + gate * update).astype(jnp.bfloat16)


def shards(
    pair,
    pair_mask,
    out_in_gain,
    out_proj,
    out_mid_gain,
    out_final,
    in_in_gain,
    in_proj,
    in_mid_gain,
    in_final,
):
    left, right, gate = project(
        pair, pair_mask, out_in_gain, out_proj, "rqd,de->erq", "rqd,de->erq", False
    )
    left, right = (
        lax.all_to_all(left, "chan", split_axis=0, concat_axis=2, tiled=True),
        lax.all_to_all(right, "chan", split_axis=0, concat_axis=2, tiled=True),
    )
    product = jnp.einsum(
        "cik,cjk->cij",
        left,
        lax.all_gather(right, ("row", "sub"), axis=1, tiled=True),
        preferred_element_type=jnp.float32,
    )
    middle = finish(pair, product, gate, out_mid_gain, out_final)
    left_in, right_in, gate_in = project(
        middle, pair_mask, in_in_gain, in_proj, "rqd,de->eqr", "rqd,de->erq", True
    )
    columns = lax.all_to_all(
        lax.all_to_all(left_in, "chan", split_axis=0, concat_axis=1, tiled=True),
        ("row", "sub"),
        split_axis=1,
        concat_axis=2,
        tiled=True,
    )
    right_in = lax.all_to_all(right_in, "chan", split_axis=0, concat_axis=2, tiled=True)
    product_in = jnp.einsum(
        "cik,ckj->cij",
        columns,
        lax.all_gather(right_in, ("row", "sub"), axis=1, tiled=True),
        preferred_element_type=jnp.float32,
    )
    return finish(middle, product_in, gate_in, in_mid_gain, in_final)


def solution(mesh):
    placed = (
        P(("parts", "row", "sub"), "chan", None),
        P(("parts", "row", "sub"), "chan"),
        P(),
        P(),
        P(),
        P(),
        P(),
        P(),
        P(),
        P(),
    )
    return jax.shard_map(
        shards,
        mesh=mesh,
        in_specs=placed,
        out_specs=P(("parts", "row", "sub"), "chan", None),
        check_vma=False,
    )
```

profile of v0, /device:TPU:0, one launch (start us, length us, event | category | flops | bytes accessed | tf_op | source)
XLA Modules:
  0.0 842.3 jit_solution(12634183757078182451)
XLA Ops:
  6.6 2.1 convert_reduce_fusion.1
  8.7 3.1 fusion.7
  11.9 1.9 convolution_bitcast_fusion.3
  13.8 1.9 convolution_bitcast_fusion.2
  15.7 2.9 fusion.23
  18.9 3.2 copy.24
  22.1 279.2 %all-gather.3.cloned.1.call-done = bf16[128,448,448]{0,2,1:T(8,128)(2,1)} async-done(((bf16[128,14,448]{0,2,1:T(8,128)(2,1)}), bf16[128,448,448]{0,2,1:T(8,128)(2,1)}) %all-gather.3.cloned.1.call-update) | async-done | bytes 51380240 | tf_op jit(solution)/shard_map/all_gather | solution.py:85
  301.4 79.1 %copy.25 = bf16[128,448,448]{2,1,0:T(8,128)(2,1)} copy(bf16[128,448,448]{0,2,1:T(8,128)(2,1)} %all-gather.3.cloned.1.call-done) | data formatting | bytes 102760448 | tf_op jit(solution)/shard_map/all_gather | solution.py:85
  380.5 23.2 %fusion.63 = (bf16[14,448]{1,0:T(8,128)(2,1)S(1)}, bf16[14,448]{1,0:T(8,128)(2,1)S(1)}, f32[128,14,448]{2,1,0:T(8,128)S(1)}) fusion(bf16[128,14,448]{2,1,0:T(8,128)(2,1)} %copy.24, bf16[128,448,448]{2,1,0:T(8,128)(2,1)} %copy.25), kind=kOutput, calls=%fused_computation.84 | convolution fusion | flops 721719040 | bytes 56222208 | tf_op jit(solution)/shard_map/cik,cjk->cij/dot_general | solution.py:82
  404.2 2.2 fusion.36
  406.5 2.9 convert_reduce_fusion
  409.4 2.0 fusion.4
  411.4 1.9 convolution_bitcast_fusion
  413.3 1.9 fusion.13
  415.2 1.9 convolution_bitcast_fusion.1
  417.1 1.4 fusion.18
  419.6 80.0 %all_to_all.18 = bf16[128,448,14]{0,2,1:T(8,128)(2,1)S(1)} all-to-all(bf16[128,448,14]{0,2,1:T(8,128)(2,1)S(1)} %copy.27), channel_id=1, replica_groups=mesh['parts'=1,'row'=16,'chan'=1,'sub'=2] {'row','sub'}, dimensions={1} | all-to-all | bytes 3211264 | tf_op jit(solution)/shard_map/all_to_all | solution.py:92
  500.0 1.4 all_to_all.16
  501.4 3.7 copy.30
  505.1 224.0 %all-gather.5.cloned.1.call-done = bf16[128,448,448]{0,2,1:T(8,128)(2,1)} async-done(((bf16[128,14,448]{0,2,1:T(8,128)(2,1)}), bf16[128,448,448]{0,2,1:T(8,128)(2,1)}) %all-gather.5.cloned.1.call-update) | async-done | bytes 51380240 | tf_op jit(solution)/shard_map/all_gather | solution.py:103
  729.1 79.1 %copy.31 = bf16[128,448,448]{2,1,0:T(8,128)(2,1)} copy(bf16[128,448,448]{0,2,1:T(8,128)(2,1)} %all-gather.5.cloned.1.call-done) | data formatting | bytes 102760448 | tf_op jit(solution)/shard_map/all_gather | solution.py:103
  808.2 20.7 %fusion.62 = (bf16[14,448]{1,0:T(8,128)(2,1)S(1)}, bf16[14,448]{1,0:T(8,128)(2,1)S(1)}, f32[128,14,448]{2,1,0:T(8,128)S(1)}) fusion(bf16[128,14,448]{2,1,0:T(8,128)(2,1)S(1)} %copy.30, bf16[128,448,448]{2,1,0:T(8,128)(2,1)} %copy.31), kind=kOutput, calls=%fused_computation.83 | convolution fusion | flops 721719040 | bytes 56222208 | tf_op jit(solution)/shard_map/cik,ckj->cij/dot_general | solution.py:100
  829.7 2.2 fusion.39
  831.9 3.5 fusion.11
  (43 shorter events, 3.2 us)
Async XLA Ops:
  6.5 397.7 %copy-start = (bf16[128,128]{1,0:T(8,128)(2,1)S(1)}, bf16[128,128]{1,0:T(8,128)(2,1)}, u32[]{:S(2)}) copy-start(bf16[128,128]{1,0:T(8,128)(2,1)} %param.15) | copy-start | bytes 98308
  6.5 5.3 copy-start.2
  6.5 5.3 copy-start.12
  6.5 5.4 copy-start.10
  6.5 294.8 %all-gather.3.cloned.1.call-start = ((), (), s32[]{:S(2)}) async-start(), calls=%async_computation.1 | async-start | bytes 52985856 | tf_op jit(solution)/shard_map/all_gather | solution.py:85
  13.8 1.9 copy-start.7
  18.6 710.5 %all-gather.5.cloned.1.call-start = ((), (), s32[]{:S(2)}) async-start(), calls=%async_computation.2 | async-start | bytes 52985856 | tf_op jit(solution)/shard_map/all_gather | solution.py:103
  380.5 23.2 %copy-start.8 = (f32[128]{0:T(128)S(1)}, f32[128]{0:T(128)}, u32[]{:S(2)}) copy-start(f32[128]{0:T(128)} %param.14) | copy-start | bytes 1540
  404.2 2.2 copy-start.3
  406.4 5.0 copy-start.11
  406.5 5.0 copy-start.13
  409.3 5.9 copy-start.4
  808.2 20.8 %copy-start.9 = (f32[128]{0:T(128)S(1)}, f32[128]{0:T(128)}, u32[]{:S(2)}) copy-start(f32[128]{0:T(128)} %param.18) | copy-start | bytes 1540
  829.0 0.8 copy-start.6
  829.7 2.2 copy-start.5
  831.9 3.5 copy-start.1
Sparse Core Ops, SparseCore 0:
  18.8 282.5 all-gather.2
  415.4 313.7 all-gather.4
where the time goes:
time: 846 us; the launch traced here: 842 us
  waiting for transfers between devices  503 us (59%)
  local copies, waits for them, and re-layouts  168 us (20%)
  blocking collectives  80 us (9%)
  matrix products  62.1 us (7%)
  other arithmetic  14.6 us (2%)
  between operations  13.7 us (2%)
    all_gather x1, waiting for transfers between devices, shards(): lax.all_gather(right, ('row', 'sub'), axis=1, tiled=True)  279 us
    all_gather x1, waiting for transfers between devices, shards(): lax.all_gather(right_in, ('row', 'sub'), axis=1, tiled=True)  224 us
    all_to_all x1, blocking collectives, shards(): lax.all_to_all(lax.all_to_all(left_in, 'chan', split_axis=0, concat_axis=...  80 us
    all_gather x1, local copies, waits for them, and re-layouts, shards(): lax.all_gather(right, ('row', 'sub'), axis=1, tiled=True)  79.1 us
    all_gather x1, local copies, waits for them, and re-layouts, shards(): lax.all_gather(right_in, ('row', 'sub'), axis=1, tiled=True)  79.1 us
    dot_general x1, matrix products, shards(): jnp.einsum('cik,cjk->cij', left, lax.all_gather(right, ('row', 'sub'), ax...  23.2 us
    dot_general x1, matrix products, shards(): jnp.einsum('cik,ckj->cij', columns, lax.all_gather(right_in, ('row', 'sub...  20.7 us
  transfers between devices with their start and end apart: 2, of which 2 were waited for; matrix products, arithmetic and copies ran while one was open for 1% of the time, Pallas kernels for 0%

commit v1 on v0

--- a/solution.py
+++ b/solution.py
@@ -100,7 +100,12 @@
     product_in = jnp.einsum(
         "cik,ckj->cij",
         columns,
-        lax.all_gather(right_in, ("row", "sub"), axis=1, tiled=True),
+        jnp.concatenate(
+            lax.all_to_all(
+                jnp.stack([right_in] * lax.axis_size(("row", "sub"))), ("row", "sub"), 0, 0
+            ),
+            axis=1,
+        ),
         preferred_element_type=jnp.float32,
     )
     return finish(middle, product_in, gate_in, in_mid_gain, in_final)

time: 846 us -> 1750 us (2.07)
  waiting for transfers between devices: 503 us -> 1460 us
  blocking collectives: 80 us -> 0 us
  local copies, waits for them, and re-layouts: 168 us -> 189 us
    all_to_all x0 -> x2, waiting for transfers between devices: none -> 1180 us  [the longest x1 1140 us: shards(): lax.all_to_all(jnp.stack([right_in] * lax.axis_size(('row', 'sub'))), ('r...]
    all_gather x1 -> x0, waiting for transfers between devices: 224 us -> none  [shards(): lax.all_gather(right_in, ('row', 'sub'), axis=1, tiled=True)]
    all_to_all x1 -> x0, blocking collectives: 80 us -> none  [shards(): lax.all_to_all(lax.all_to_all(left_in, 'chan', split_axis=0, concat_axis=...]
    all_gather x1 -> x0, local copies, waits for them, and re-layouts: 79.1 us -> none  [shards(): lax.all_gather(right_in, ('row', 'sub'), axis=1, tiled=True)]
    reshape x0 -> x1, local copies, waits for them, and re-layouts: none -> 78.8 us  [shards(): jnp.concatenate(lax.all_to_all(jnp.stack([right_in] * lax.axis_size(('row...]
  transfers between devices with their start and end apart: 2 -> 3, of which waited for: 2 -> 3; matrix products, arithmetic and copies ran while one was open for 1% -> 1% of each run, Pallas kernels for 0% -> 0%
where the time goes in v1:
time: 1750 us
  waiting for transfers between devices  1460 us (83%)
  local copies, waits for them, and re-layouts  189 us (11%)
  matrix products  65.3 us (4%)
    all_to_all x1, waiting for transfers between devices, shards(): lax.all_to_all(jnp.stack([right_in] * lax.axis_size(('row', 'sub'))), ('r...  1140 us
    all_gather x1, waiting for transfers between devices, shards(): lax.all_gather(right, ('row', 'sub'), axis=1, tiled=True)  279 us
    reshape x1, local copies, waits for them, and re-layouts, shards(): jnp.concatenate(lax.all_to_all(jnp.stack([right_in] * lax.axis_size(('row...  78.8 us
    all_gather x1, local copies, waits for them, and re-layouts, shards(): lax.all_gather(right, ('row', 'sub'), axis=1, tiled=True)  78.8 us
    all_to_all x1, waiting for transfers between devices, shards(): lax.all_to_all(lax.all_to_all(left_in, 'chan', split_axis=0, concat_axis=...  39.2 us
  transfers between devices with their start and end apart: 3, of which 3 were waited for; matrix products, arithmetic and copies ran while one was open for 1% of the time, Pallas kernels for 0%

profile of v1, /device:TPU:0, one launch (start us, length us, event | category | flops | bytes accessed | tf_op | source)
XLA Modules:
  0.0 1749.8 jit_solution(7985218156106140852)
XLA Ops:
  6.6 2.1 convert_reduce_fusion.1
  8.7 3.1 fusion.7
  15.7 2.9 fusion.23
  18.7 3.2 copy.24
  21.9 279.5 %all-gather.2.cloned.1.call-done = bf16[128,448,448]{0,2,1:T(8,128)(2,1)} async-done(((bf16[128,14,448]{0,2,1:T(8,128)(2,1)}), bf16[128,448,448]{0,2,1:T(8,128)(2,1)}) %all-gather.2.cloned.1.call-update) | async-done | bytes 51380240 | tf_op jit(solution)/shard_map/all_gather | solution.py:85
  301.4 78.8 %copy.25 = bf16[128,448,448]{2,1,0:T(8,128)(2,1)} copy(bf16[128,448,448]{0,2,1:T(8,128)(2,1)} %all-gather.2.cloned.1.call-done) | data formatting | bytes 102760448 | tf_op jit(solution)/shard_map/all_gather | solution.py:85
  380.2 23.2 %fusion.63 = (bf16[14,448]{1,0:T(8,128)(2,1)S(1)}, bf16[14,448]{1,0:T(8,128)(2,1)S(1)}, f32[128,14,448]{2,1,0:T(8,128)S(1)}) fusion(bf16[128,14,448]{2,1,0:T(8,128)(2,1)} %copy.24, bf16[128,448,448]{2,1,0:T(8,128)(2,1)} %copy.25), kind=kOutput, calls=%fused_computation.84 | convolution fusion | flops 721719040 | bytes 56222208 | tf_op jit(solution)/shard_map/cik,cjk->cij/dot_general | solution.py:82
  404.0 2.2 fusion.36
  406.2 3.6 convert_reduce_fusion
  409.9 2.2 fusion.4
  412.1 2.7 convolution_bitcast_fusion.1
  416.0 2.3 copy.27
  418.3 2.8 all-to-all-start
  421.1 2.7 convolution_bitcast_fusion
  425.0 39.2 %all-to-all-done = bf16[128,448,14]{0,2,1:T(8,128)(2,1)S(1)} async-done(((bf16[128,448,14]{0,2,1:T(8,128)(2,1)}), bf16[128,448,14]{0,2,1:T(8,128)(2,1)S(1)}, u32[]{:S(2)}, u32[]{:S(2)}) %all-to-all-start) | async-done | bytes 1605664 | tf_op jit(solution)/shard_map/all_to_all | solution.py:92
  464.2 16.4 stack.2
  480.6 4.9 all-to-all-start.1
  487.2 3.6 all_to_all.19
  490.9 3.5 copy.30
  494.4 1141.8 %all-to-all-done.1 = bf16[32,128,14,448]{1,3,2,0:T(8,128)(2,1)} async-done(((bf16[32,128,14,448]{1,3,2,0:T(8,128)(2,1)}), bf16[32,128,14,448]{1,3,2,0:T(8,128)(2,1)}, u32[]{:S(2)}, u32[]{:S(2)}) %all-to-all-start.1) | async-done | bytes 51380256 | tf_op jit(solution)/shard_map/all_to_all | solution.py:104
  1636.2 78.8 %copy.31 = bf16[128,448,448]{2,1,0:T(8,128)(2,1)} copy(bf16[128,448,448]{0,2,1:T(8,128)(2,1)} %bitcast.16) | data formatting | bytes 102760448 | tf_op jit(solution)/shard_map/reshape | solution.py:103
  1715.0 20.7 %fusion.62 = (bf16[14,448]{1,0:T(8,128)(2,1)S(1)}, bf16[14,448]{1,0:T(8,128)(2,1)S(1)}, f32[128,14,448]{2,1,0:T(8,128)S(1)}) fusion(bf16[128,14,448]{2,1,0:T(8,128)(2,1)S(1)} %copy.30, bf16[128,448,448]{2,1,0:T(8,128)(2,1)} %copy.31), kind=kOutput, calls=%fused_computation.83 | convolution fusion | flops 721719040 | bytes 56222208 | tf_op jit(solution)/shard_map/cik,ckj->cij/dot_general | solution.py:100
  1736.5 2.2 fusion.39
  1738.7 4.3 fusion.11
  (58 shorter events, 9.1 us)
Async XLA Ops:
  6.5 397.4 %copy-start = (bf16[128,128]{1,0:T(8,128)(2,1)S(1)}, bf16[128,128]{1,0:T(8,128)(2,1)}, u32[]{:S(2)}) copy-start(bf16[128,128]{1,0:T(8,128)(2,1)} %param.15) | copy-start | bytes 98308
  6.5 5.3 copy-start.2
  6.5 5.4 copy-start.19
  6.5 5.4 copy-start.18
  6.5 294.8 %all-gather.2.cloned.1.call-start = ((), (), s32[]{:S(2)}) async-start(), calls=%async_computation.2 | async-start | bytes 52985856 | tf_op jit(solution)/shard_map/all_gather | solution.py:85
  8.7 5.1 copy-start.8
  11.9 1.9 copy-start.14
  13.8 1.9 copy-start.11
  380.2 23.2 %copy-start.16 = (f32[128]{0:T(128)S(1)}, f32[128]{0:T(128)}, u32[]{:S(2)}) copy-start(f32[128]{0:T(128)} %param.14) | copy-start | bytes 1540
  403.9 2.2 copy-start.3
  404.0 2.2 copy-start.9
  404.0 2.2 copy-start.15
  406.2 5.9 copy-start.20
  409.9 11.3 copy-start.4
  409.9 11.2 copy-start.6
  412.1 2.7 copy-start.12
  416.0 5.1 copy-start.13
  418.3 45.9 %all-to-all-start = ((bf16[128,448,14]{0,2,1:T(8,128)(2,1)}), bf16[128,448,14]{0,2,1:T(8,128)(2,1)S(1)}, u32[]{:S(2)}, u32[]{:S(2)}) async-start(bf16[128,448,14]{0,2,1:T(8,128)(2,1)} %copy.27), calls=%async_computation | async-start | bytes 3670016 | tf_op jit(solution)/shard_map/all_to_all | solution.py:92
  480.6 1155.6 %all-to-all-start.1 = ((bf16[32,128,14,448]{1,3,2,0:T(8,128)(2,1)}), bf16[32,128,14,448]{1,3,2,0:T(8,128)(2,1)}, u32[]{:S(2)}, u32[]{:S(2)}) async-start(bf16[32,128,14,448]{1,3,2,0:T(8,128)(2,1)} %stack.2), calls=%async_computation.1 | async-start | bytes 102760448 | tf_op jit(solution)/shard_map/all_to_all | solution.py:104
  1715.0 20.8 %copy-start.17 = (f32[128]{0:T(128)S(1)}, f32[128]{0:T(128)}, u32[]{:S(2)}) copy-start(f32[128]{0:T(128)} %param.18) | copy-start | bytes 1540
  1735.7 0.8 copy-start.10
  1736.5 2.2 copy-start.5
  1736.5 2.2 copy-start.7
  1738.7 4.3 copy-start.1
Sparse Core Ops, SparseCore 0:
  18.8 282.5 all-gather.1
